TPU v7x, 32 devices: a whole 2x2x4 slice. The times are simulated.
32 devices in a mesh: psg: 8 (over y, x, core), qry: 4 (over z).
Axes of the slice: x: 2, y: 2, z: 4, core: 2. Of those that a mesh axis runs over, the one named last changes fastest.
Arguments:
- hidden: bfloat16 [512, 4096], P('qry'), may hold values from -6 to 6
- norm_gain: float32 [4096], replicated, may hold values from 0.5 to 1.5
- proj_weight: bfloat16 [4096, 4096], P('psg', 'qry'), may hold values from -0.09375 to 0.09375
- pq_codes: int32 [16384, 512], P('psg', 'qry'), may hold values from 0 to 255
- codebook: bfloat16 [512, 8, 256], P('qry'), may hold values from -560 to 560
- positives: int32 [512], replicated, may hold values from 0 to 16383
Outputs:
- losses: float32 [512], P('qry')
- hidden_grad: bfloat16 [512, 4096], P('qry')
- weight_grad: float32 [4096, 4096], P('psg', 'qry')
- codebook_grad: float32 [512, 8, 256], P('qry')
All inputs are finite; a program needn't handle non-finite values.
Results may differ from a plain program's by a relative error of at most 0.019.
The roundings to bfloat16 on the way count: a program that leaves them out, or rounds other values in their place, can miss the bound.
Values may be sent and summed in bfloat16 or wider, within the bound.
No kernel may reach another device: no remote copies, remote signals or barrier semaphores. Data moves between devices by JAX's collectives and lax.ppermute only.
A program may use at most 128 MiB of HBM per device.

v0:
```python
import jax
import jax.numpy as jnp
from jax import lax
from jax.sharding import PartitionSpec as P

score_scale = 0.0625
norm_eps = 1e-06


def code_hot(code_block, book):
    levels = lax.broadcasted_iota(jnp.int32, code_block.shape + (book.shape[2],), 2)
    return (code_block[:, :, None] == levels).astype(jnp.bfloat16)


def per_device(hidden, norm_gain, proj_weight, pq_codes, codebook, positives):
    gathered = lax.all_gather(hidden, "qry", axis=0, tiled=True)
    floats_all = gathered.astype(jnp.float32)
    inverse_all = lax.rsqrt(jnp.mean(floats_all * floats_all, axis=1, keepdims=True) + norm_eps)
    normed = (floats_all * inverse_all * norm_gain[None, :]).astype(jnp.bfloat16)
    columns = proj_weight.shape[1]
    query_float = jnp.dot(
        normed,
        lax.all_gather(proj_weight, "psg", axis=0, tiled=True),
        preferred_element_type=jnp.float32,
    )
    queries = query_float.astype(jnp.bfloat16)
    passage_count = pq_codes.shape[0]
    sub_count = codebook.shape[0]
    sub_width = codebook.shape[1]
    block_rows = min(passage_count, 512)
    code_blocks = pq_codes.reshape(passage_count // block_rows, block_rows, sub_count)

    def decode(code_block):
        hot_table = code_hot(code_block, codebook)
        vectors = jnp.einsum(
            "pmk,mdk->pmd", hot_table, codebook, preferred_element_type=jnp.float32
        )
        return vectors.astype(jnp.bfloat16).reshape(block_rows, columns)

    passages = lax.map(decode, code_blocks).reshape(passage_count, columns)
    partial_value = (
        lax.dot_general(
            queries, passages, (((1,), (1,)), ((), ())), preferred_element_type=jnp.float32
        )
        * score_scale
    )
    qry_index = lax.axis_index("qry")
    own_rows = hidden.shape[0]
    scores = lax.psum_scatter(partial_value, "qry", scatter_dimension=0, tiled=True)
    row_targets = lax.dynamic_slice_in_dim(positives, qry_index * own_rows, own_rows, 0)
    local_target = row_targets - lax.axis_index("psg") * passage_count
    target = lax.broadcasted_iota(jnp.int32, scores.shape, 1) == local_target[:, None]
    local_max = jnp.max(scores, axis=1)
    positive_part = jnp.sum(jnp.where(target, scores, 0.0), axis=1)
    row_max = lax.pmax(local_max, "psg")
    shifted_total = jnp.sum(jnp.exp(scores - row_max[:, None]), axis=1)
    row_total, positive_score = lax.psum((shifted_total, positive_part), "psg")
    losses = jnp.log(row_total) + row_max - positive_score
    score_grad = (
        jnp.exp(scores - row_max[:, None]) / row_total[:, None] - target.astype(jnp.float32)
    ).astype(jnp.bfloat16)
    all_grad = lax.all_gather(score_grad, "qry", axis=0, tiled=True)
    query_part = jnp.dot(all_grad, passages, preferred_element_type=jnp.float32) * score_scale
    query_grad = lax.psum(query_part, "psg").astype(jnp.bfloat16)
    passage_grad = (
        lax.dot_general(
            all_grad, queries, (((0,), (0,)), ((), ())), preferred_element_type=jnp.float32
        )
        * score_scale
    ).astype(jnp.bfloat16)
    grad_blocks = passage_grad.reshape(
        passage_count // block_rows, block_rows, sub_count, sub_width
    )

    def add_book(carry, paired):
        code_block, grad_block = paired
        hot_table = code_hot(code_block, codebook)
        return (
            carry
            + jnp.einsum("pmk,pmd->mdk", hot_table, grad_block, preferred_element_type=jnp.float32),
            None,
        )

    book_part, unused = lax.scan(
        add_book, jnp.zeros(codebook.shape, jnp.float32), (code_blocks, grad_blocks)
    )
    codebook_grad = lax.psum(book_part.astype(jnp.bfloat16), "psg").astype(jnp.float32)
    row_span = proj_weight.shape[0]
    normed_rows = lax.dynamic_slice_in_dim(normed, lax.axis_index("psg") * row_span, row_span, 1)
    weight_grad = lax.dot_general(
        normed_rows, query_grad, (((0,), (0,)), ((), ())), preferred_element_type=jnp.float32
    )
    norm_part = lax.dot_general(
        query_grad,
        lax.all_gather(proj_weight, "psg", axis=0, tiled=True),
        (((1,), (1,)), ((), ())),
        preferred_element_type=jnp.float32,
    )
    norm_back = lax.psum_scatter(
        norm_part.astype(jnp.bfloat16), "qry", scatter_dimension=0, tiled=True
    ).astype(jnp.float32)
    floats_own = hidden.astype(jnp.float32)
    inverse_own = lax.rsqrt(jnp.mean(floats_own * floats_own, axis=1, keepdims=True) + norm_eps)
    scaled = norm_back * norm_gain[None, :]
    hidden_grad = (
        inverse_own * scaled
        - floats_own
        * inverse_own
        * inverse_own
        * inverse_own
        * jnp.mean(scaled * floats_own, axis=1, keepdims=True)
    ).astype(jnp.bfloat16)
    return (losses, hidden_grad, weight_grad, codebook_grad)


def solution(mesh):
    in_specs = (P("qry", None), P(), P("psg", "qry"), P("psg", "qry"), P("qry", None, None), P())
    out_specs = (P("qry"), P("qry", None), P("psg", "qry"), P("qry", None, None))
    return jax.shard_map(
        per_device, mesh=mesh, in_specs=in_specs, out_specs=out_specs, check_vma=False
    )
```

profile of v0, /device:TPU:0, one launch (start us, length us, event | category | flops | bytes accessed | tf_op | source)
XLA Modules:
  0.0 560.6 jit_solution(67081673315906071)
XLA Ops:
  7.2 0.7 all-gather.4.cloned.1.call-update
  7.9 0.7 all-gather.6.cloned.1.call-update
  8.7 1.6 copy.11
  10.3 61.1 %while.21 = (s32[]{:T(128)}, bf16[4,512,1024]{2,1,0:T(8,128)(2,1)}, s32[4,512,128]{1,2,0:T(8,128)S(1)}, bf16[128,8,256]{2,1,0:T(8,128)(2,1)}, s32[]{:T(128)}) while((s32[]{:T(128)}, bf16[4,512,1024]{2,1,0:T(8,128)(2,1)}, s32[4,512,128]{1,2,0:T(8,128)S(1)}, bf16[128,8,256]{2,1,0:T(8,128)(2,1)}, s32[]{:T(128)}) %tuple.45), condition=%wide.region_2.3_spmd, body=%wide.region_1.2_spmd.sunk | while | flops 285736960 | bytes 6553677 | solution.py:40
  10.3 13.6 %fusion.47 = bf16[1,512,1024]{1,2,0:T(8,128)(2,1)S(1)} fusion(bf16[128,8,256]{2,1,0:T(8,128)(2,1)} %get-tuple-element.164, s32[512,128]{0,1:T(8,128)S(1)} %dynamic-slice_bitcast_fusion.4), kind=kOutput, calls=%fused_computation.4.clone.2 | convolution fusion | flops 285736960 | bytes 1835008 | tf_op jit(solution)/shard_map/while/body/eval_jaxpr/pmk,mdk->pmd/dot_general | solution.py:35
  24.0 0.5 copy.19
  24.5 1.1 constant_dynamic-update-slice_fusion.2
  25.7 13.6 %fusion.47 = bf16[1,512,1024]{1,2,0:T(8,128)(2,1)S(1)} fusion(bf16[128,8,256]{2,1,0:T(8,128)(2,1)} %get-tuple-element.164, s32[512,128]{0,1:T(8,128)S(1)} %dynamic-slice_bitcast_fusion.4), kind=kOutput, calls=%fused_computation.4.clone.2 | convolution fusion | flops 285736960 | bytes 1835008 | tf_op jit(solution)/shard_map/while/body/eval_jaxpr/pmk,mdk->pmd/dot_general | solution.py:35
  39.8 1.0 constant_dynamic-update-slice_fusion.2
  40.9 13.6 %fusion.47 = bf16[1,512,1024]{1,2,0:T(8,128)(2,1)S(1)} fusion(bf16[128,8,256]{2,1,0:T(8,128)(2,1)} %get-tuple-element.164, s32[512,128]{0,1:T(8,128)S(1)} %dynamic-slice_bitcast_fusion.4), kind=kOutput, calls=%fused_computation.4.clone.2 | convolution fusion | flops 285736960 | bytes 1835008 | tf_op jit(solution)/shard_map/while/body/eval_jaxpr/pmk,mdk->pmd/dot_general | solution.py:35
  54.5 0.5 copy.19
  55.1 1.1 constant_dynamic-update-slice_fusion.2
  56.2 13.6 %fusion.47 = bf16[1,512,1024]{1,2,0:T(8,128)(2,1)S(1)} fusion(bf16[128,8,256]{2,1,0:T(8,128)(2,1)} %get-tuple-element.164, s32[512,128]{0,1:T(8,128)S(1)} %dynamic-slice_bitcast_fusion.4), kind=kOutput, calls=%fused_computation.4.clone.2 | convolution fusion | flops 285736960 | bytes 1835008 | tf_op jit(solution)/shard_map/while/body/eval_jaxpr/pmk,mdk->pmd/dot_general | solution.py:35
  70.3 1.1 constant_dynamic-update-slice_fusion.2
  71.4 21.8 %all-gather.4.cloned.1.call-done = bf16[512,4096]{1,0:T(8,128)(2,1)} async-done(((bf16[128,4096]{1,0:T(8,128)(2,1)}), bf16[512,4096]{1,0:T(8,128)(2,1)}) %all-gather.4.cloned.1.call-update) | async-done | bytes 4194320 | tf_op jit(solution)/shard_map/all_gather | solution.py:16
  93.2 3.2 fusion.10
  96.6 3.6 fusion.12
  100.2 47.6 %all-gather.6.cloned.1.call-done = bf16[4096,1024]{1,0:T(8,128)(2,1)} async-done(((bf16[512,1024]{1,0:T(8,128)(2,1)}), bf16[4096,1024]{1,0:T(8,128)(2,1)}) %all-gather.6.cloned.1.call-update) | async-done | bytes 8388624 | tf_op jit(solution)/shard_map/all_gather | solution.py:23
  147.8 9.3 %convolution_convert_fusion.1 = bf16[512,1024]{1,0:T(8,128)(2,1)S(1)} fusion(bf16[512,4096]{1,0:T(8,128)(2,1)} %fusion.12, bf16[4096,1024]{1,0:T(8,128)(2,1)} %all-gather.6.cloned.1.call-done), kind=kOutput, calls=%fused_computation.35 | convolution fusion | flops 4295491584 | bytes 13631488 | tf_op jit(solution)/shard_map/dot_general | solution.py:21
  157.1 1.0 copy-done.7
  158.1 4.3 convolution_multiply_fusion
  162.5 0.8 dynamic-slice_subtract_fusion
  163.2 76.1 %reduce-scatter.3.cloned.1.call-done = f32[128,2048]{1,0:T(8,128)} async-done(((f32[512,2048]{1,0:T(8,128)}), f32[128,2048]{1,0:T(8,128)}) %reduce-scatter.3.cloned.1.call-update) | async-done | bytes 1048592 | tf_op jit(solution)/shard_map/reduce_scatter | solution.py:49
  239.4 1.4 reduce_max.9
  240.7 13.3 %pmax.7 = f32[128]{0:T(128)S(1)} all-reduce(f32[128]{0:T(128)S(1)} %reduce_max.9), channel_id=1, replica_groups=mesh['psg'=8,'qry'=4] {'psg'}, use_global_device_ids=true, to_apply=%region_5.6 | all-reduce | flops 128 | bytes 1024 | tf_op jit(solution)/shard_map/pmax | solution.py:55
  254.0 1.6 fusion.20
  255.6 11.8 %psum.28 = f32[128]{0:T(128)S(1)} all-reduce(f32[128]{0:T(128)S(1)} %get-tuple-element.79), channel_id=1, replica_groups=mesh['psg'=8,'qry'=4] {'psg'}, use_global_device_ids=true, to_apply=%region_7.8 | all-reduce | flops 128 | bytes 1024 | tf_op jit(solution)/shard_map/psum | solution.py:57
  267.4 2.4 subtract_convert_fusion
  270.1 44.5 %all-gather.8.cloned.1.call-done = bf16[512,2048]{1,0:T(8,128)(2,1)} async-done(((bf16[128,2048]{1,0:T(8,128)(2,1)}), bf16[512,2048]{1,0:T(8,128)(2,1)}) %all-gather.8.cloned.1.call-update) | async-done | bytes 2097168 | tf_op jit(solution)/shard_map/all_gather | solution.py:62
  314.7 5.3 convolution_multiply_fusion.1
  320.0 4.3 multiply_convert_fusion
  324.3 6.5 %copy.13 = bf16[2048,1024]{0,1:T(8,128)(2,1)} copy(bf16[2048,1024]{1,0:T(8,128)(2,1)} %multiply_convert_fusion) | data formatting | bytes 8388608 | tf_op jit(solution)/shard_map/convert_element_type | solution.py:70
  330.8 7.8 %reshape.49 = bf16[4,512,128,8]{1,0,3,2:T(4,128)(2,1)} reshape(bf16[2048,1024]{0,1:T(8,128)(2,1)} %copy.13) | data formatting | bytes 8388608 | tf_op jit(solution)/shard_map/reshape | solution.py:71
  338.6 5.0 copy.14
  343.6 57.8 %while.22 = (s32[]{:T(128)}, f32[128,8,256]{2,1,0:T(8,128)}, bf16[4,512,128,8]{1,3,2,0:T(8,128)(2,1)}, s32[4,512,128]{1,2,0:T(8,128)S(1)}, s32[]{:T(128)}, /*index=5*/s32[]{:T(128)}) while((s32[]{:T(128)}, f32[128,8,256]{2,1,0:T(8,128)}, bf16[4,512,128,8]{1,3,2,0:T(8,128)(2,1)}, s32[4,512,128]{1,2,0:T(8,128)S(1)}, s32[]{:T(128)}, ...), condition=%wide.region_15.16_spmd.clone, body=%wide.region_14.15_spmd.clone.sunk | while | flops 285736960 | bytes 3932255 | solution.py:84
  343.6 14.4 %fusion.49 = f32[128,8,256]{2,1,0:T(8,128)} fusion(s32[512,128]{0,1:T(8,128)S(1)} %dynamic-slice_bitcast_fusion.5, f32[128,8,256]{2,1,0:T(8,128)} %get-tuple-element.173, bf16[4,512,128,8]{1,3,2,0:T(8,128)(2,1)} %get-tuple-element.180, s32[]{:T(128)S(6)} %copy.31, pred[]{:T(512)S(6)} %compare.3), kind=kOutput, calls=%fused_computation.10.clone.3 | convolution fusion | flops 285736960 | bytes 3407877 | tf_op jit(solution)/shard_map/while/body/eval_jaxpr/pmk,pmd->mdk/dot_general | solution.py:80
  358.1 14.4 %fusion.49 = f32[128,8,256]{2,1,0:T(8,128)} fusion(s32[512,128]{0,1:T(8,128)S(1)} %dynamic-slice_bitcast_fusion.5, f32[128,8,256]{2,1,0:T(8,128)} %get-tuple-element.173, bf16[4,512,128,8]{1,3,2,0:T(8,128)(2,1)} %get-tuple-element.180, s32[]{:T(128)S(6)} %copy.31, pred[]{:T(512)S(6)} %compare.3), kind=kOutput, calls=%fused_computation.10.clone.3 | convolution fusion | flops 285736960 | bytes 3407877 | tf_op jit(solution)/shard_map/while/body/eval_jaxpr/pmk,pmd->mdk/dot_general | solution.py:80
  372.5 14.4 %fusion.49 = f32[128,8,256]{2,1,0:T(8,128)} fusion(s32[512,128]{0,1:T(8,128)S(1)} %dynamic-slice_bitcast_fusion.5, f32[128,8,256]{2,1,0:T(8,128)} %get-tuple-element.173, bf16[4,512,128,8]{1,3,2,0:T(8,128)(2,1)} %get-tuple-element.180, s32[]{:T(128)S(6)} %copy.31, pred[]{:T(512)S(6)} %compare.3), kind=kOutput, calls=%fused_computation.10.clone.3 | convolution fusion | flops 285736960 | bytes 3407877 | tf_op jit(solution)/shard_map/while/body/eval_jaxpr/pmk,pmd->mdk/dot_general | solution.py:80
  387.0 14.4 %fusion.49 = f32[128,8,256]{2,1,0:T(8,128)} fusion(s32[512,128]{0,1:T(8,128)S(1)} %dynamic-slice_bitcast_fusion.5, f32[128,8,256]{2,1,0:T(8,128)} %get-tuple-element.173, bf16[4,512,128,8]{1,3,2,0:T(8,128)(2,1)} %get-tuple-element.180, s32[]{:T(128)S(6)} %copy.31, pred[]{:T(512)S(6)} %compare.3), kind=kOutput, calls=%fused_computation.10.clone.3 | convolution fusion | flops 285736960 | bytes 3407877 | tf_op jit(solution)/shard_map/while/body/eval_jaxpr/pmk,pmd->mdk/dot_general | solution.py:80
  401.4 2.1 convert_element_type.58
  403.6 60.3 %all-reduce.5 = (f32[128]{0:T(128)S(1)}, bf16[512,1024]{1,0:T(8,128)(2,1)S(1)}) all-reduce(f32[128]{0:T(128)S(1)} %get-tuple-element.80, f32[512,1024]{1,0:T(8,128)S(1)} %convolution_multiply_fusion.1), channel_id=1, replica_groups=mesh['psg'=8,'qry'=4] {'psg'}, use_global_device_ids=true, to_apply=%region_9.10 | all-reduce | flops 524416 | bytes 3146752 | tf_op jit(solution)/shard_map/psum | solution.py:57
  463.9 9.9 %convolution_convert_fusion = bf16[512,4096]{1,0:T(8,128)(2,1)} fusion(bf16[4096,1024]{1,0:T(8,128)(2,1)} %all-gather.6.cloned.1.call-done, bf16[512,1024]{1,0:T(8,128)(2,1)S(1)} %get-tuple-element.98), kind=kOutput, calls=%fused_computation.21 | convolution fusion | flops 4297064448 | bytes 13631488 | tf_op jit(solution)/shard_map/dot_general | solution.py:93
  474.3 0.7 copy-done.3
  475.0 3.1 fusion.21
  478.1 2.2 convert_element_type.59
  480.3 68.7 %reduce-scatter.5.cloned.1.call-done = bf16[128,4096]{1,0:T(8,128)(2,1)} async-done(((bf16[512,4096]{1,0:T(8,128)(2,1)}), bf16[128,4096]{1,0:T(8,128)(2,1)}) %reduce-scatter.5.cloned.1.call-update) | async-done | bytes 1048592 | tf_op jit(solution)/shard_map/reduce_scatter | solution.py:99
  549.0 1.8 fusion.13
  550.8 2.9 fusion.18
  (42 shorter events, 2.5 us)
Async XLA Ops:
  7.2 86.0 %all-gather.4.cloned.1.call-start = ((), (), s32[]{:S(2)}) async-start(), calls=%async_computation.2 | async-start | bytes 5242880 | tf_op jit(solution)/shard_map/all_gather | solution.py:16
  7.9 139.9 %all-gather.6.cloned.1.call-start = ((), (), s32[]{:S(2)}) async-start(), calls=%async_computation.3 | async-start | bytes 9437184 | tf_op jit(solution)/shard_map/all_gather | solution.py:23
  8.6 230.7 %reduce-scatter.3.cloned.1.call-start = ((), (), s32[]{:S(2)}) async-start(), calls=%async_computation.4 | async-start | bytes 5242880 | tf_op jit(solution)/shard_map/reduce_scatter | solution.py:49
  10.3 86.2 %copy-start.4 = (f32[4096]{0:T(1024)S(1)}, f32[4096]{0:T(1024)}, u32[]{:S(2)}) copy-start(f32[4096]{0:T(1024)} %param.11) | copy-start | bytes 49156
  93.2 3.4 copy-start
  147.8 10.3 %copy-start.5 = (bf16[4,512,1024]{2,1,0:T(8,128)(2,1)S(1)}, bf16[4,512,1024]{2,1,0:T(8,128)(2,1)}, u32[]{:S(2)}) copy-start(bf16[4,512,1024]{2,1,0:T(8,128)(2,1)} %get-tuple-element.48) | copy-start | bytes 12582916
  157.1 1.0 copy-start.7
  162.4 152.3 %all-gather.8.cloned.1.call-start = ((), (), s32[]{:S(2)}) async-start(), calls=%async_computation.5 | async-start | bytes 2621440 | tf_op jit(solution)/shard_map/all_gather | solution.py:62
  269.9 208.2 %all-reduce.4.cloned.1.call-start = ((), (), s32[]{:S(2)}) async-start(), calls=%async_computation.7 | async-start | bytes 1048576 | tf_op jit(solution)/shard_map/psum | solution.py:87
  314.7 5.3 copy-start.6
  314.7 5.3 copy-start.8
  403.5 145.5 %reduce-scatter.5.cloned.1.call-start = ((), (), s32[]{:S(2)}) async-start(), calls=%async_computation.6 | async-start | bytes 5242880 | tf_op jit(solution)/shard_map/reduce_scatter | solution.py:99
  463.9 9.9 %copy-start.2 = (bf16[512,1024]{1,0:T(8,128)(2,1)}, bf16[512,1024]{1,0:T(8,128)(2,1)S(1)}, u32[]{:S(2)}) copy-start(bf16[512,1024]{1,0:T(8,128)(2,1)S(1)} %get-tuple-element.98) | copy-start | bytes 3145732
  473.8 1.2 copy-start.3
  473.8 75.2 %copy-start.1 = (bf16[128,4096]{1,0:T(8,128)(2,1)S(1)}, bf16[128,4096]{1,0:T(8,128)(2,1)}, u32[]{:S(2)}) copy-start(bf16[128,4096]{1,0:T(8,128)(2,1)} %param.10) | copy-start | bytes 3145732
Sparse Core Ops, SparseCore 0:
  9.5 83.5 all-gather.3
  95.1 52.7 all-gather.5
  162.5 76.7 reduce-scatter.2
  270.0 44.5 all-gather.7
  403.7 54.7 all-reduce.3
  473.9 75.0 reduce-scatter.4
where the time goes:
time: 562 us; the launch traced here: 561 us
  waiting for transfers between devices  260 us (46%)
  matrix products  148 us (26%)
  blocking collectives  85.4 us (15%)
  local copies, waits for them, and re-layouts  29.3 us (5%)
  other arithmetic  22.6 us (4%)
  between operations  14.2 us (3%)
    reduce_scatter x1, waiting for transfers between devices, per_device(): lax.psum_scatter(partial_value, 'qry', scatter_dimension=0, tiled=True)  76.1 us
    psum x2, blocking collectives, per_device(): row_total, positive_score = lax.psum((shifted_total, positive_part), 'psg')  72.1 us
    reduce_scatter x1, waiting for transfers between devices, per_device(): lax.psum_scatter(norm_part.astype(jnp.bfloat16), 'qry', scatter_dimension...  68.7 us
    dot_general x4, matrix products, add_book(): jnp.einsum('pmk,pmd->mdk', hot_table, grad_block, preferred_element_type=...  57.7 us
    dot_general x4, matrix products, decode(): jnp.einsum('pmk,mdk->pmd', hot_table, codebook, preferred_element_type=jn...  54.6 us
    all_gather x1, waiting for transfers between devices, per_device(): lax.all_gather(proj_weight, 'psg', axis=0, tiled=True)  47.6 us
    all_gather x1, waiting for transfers between devices, per_device(): all_grad = lax.all_gather(score_grad, 'qry', axis=0, tiled=True)  44.5 us
    all_gather x1, waiting for transfers between devices, per_device(): gathered = lax.all_gather(hidden, 'qry', axis=0, tiled=True)  21.8 us
  transfers between devices with their start and end apart: 6, of which 5 were waited for; matrix products, arithmetic and copies ran while one was open for 15% of the time, Pallas kernels for 0%

commit v1 on v0

--- a/solution.py
+++ b/solution.py
@@ -20,7 +20,9 @@
     columns = proj_weight.shape[1]
     query_float = jnp.dot(
         normed,
-        lax.all_gather(proj_weight, "psg", axis=0, tiled=True),
+        jnp.concatenate(
+            lax.all_to_all(jnp.stack([proj_weight] * lax.axis_size("psg")), "psg", 0, 0), axis=0
+        ),
         preferred_element_type=jnp.float32,
     )
     queries = query_float.astype(jnp.bfloat16)

time: 562 us -> 581 us (1.034)
  matrix products: 148 us -> 158 us
    all_gather x1, waiting for transfers between devices: 47.6 us -> 0.02 us  [per_device(): lax.all_gather(proj_weight, 'psg', axis=0, tiled=True)]
    psum x1, waiting for transfers between devices: 0.01 us -> 40.1 us  [per_device(): lax.psum(book_part.astype(jnp.bfloat16), 'psg').astype(jnp.float32)]
    all_to_all x0 -> x1, waiting for transfers between devices: none -> 13.2 us  [per_device(): lax.all_to_all(jnp.stack([proj_weight] * lax.axis_size('psg')), 'psg', 0, 0)]
    all_gather x1, waiting for transfers between devices: 21.8 us -> 12.8 us  [per_device(): gathered = lax.all_gather(hidden, 'qry', axis=0, tiled=True)]
    dot_general x4, matrix products: 57.7 us -> 66.6 us  [add_book(): jnp.einsum('pmk,pmd->mdk', hot_table, grad_block, preferred_element_type=...]
    reduce_scatter x1, waiting for transfers between devices: 68.7 us -> 76.2 us  [per_device(): lax.psum_scatter(norm_part.astype(jnp.bfloat16), 'qry', scatter_dimension...]
  transfers between devices with their start and end apart: 6 -> 7, of which waited for: 5 -> 6; matrix products, arithmetic and copies ran while one was open for 15% -> 32% of each run, Pallas kernels for 0% -> 0%
where the time goes in v1:
time: 581 us; the launch traced here: 579 us
  waiting for transfers between devices  264 us (45%)
  matrix products  158 us (27%)
  blocking collectives  83 us (14%)
  local copies, waits for them, and re-layouts  33 us (6%)
  other arithmetic  21.1 us (4%)
  between operations  14.2 us (2%)
    reduce_scatter x1, waiting for transfers between devices, per_device(): lax.psum_scatter(partial_value, 'qry', scatter_dimension=0, tiled=True)  76.3 us
    reduce_scatter x1, waiting for transfers between devices, per_device(): lax.psum_scatter(norm_part.astype(jnp.bfloat16), 'qry', scatter_dimension...  76.2 us
    psum x2, blocking collectives, per_device(): row_total, positive_score = lax.psum((shifted_total, positive_part), 'psg')  69.7 us
    dot_general x4, matrix products, add_book(): jnp.einsum('pmk,pmd->mdk', hot_table, grad_block, preferred_element_type=...  66.6 us
    dot_general x4, matrix products, decode(): jnp.einsum('pmk,mdk->pmd', hot_table, codebook, preferred_element_type=jn...  54.6 us
    all_gather x1, waiting for transfers between devices, per_device(): all_grad = lax.all_gather(score_grad, 'qry', axis=0, tiled=True)  44 us
    psum x1, waiting for transfers between devices, per_device(): lax.psum(book_part.astype(jnp.bfloat16), 'psg').astype(jnp.float32)  40.1 us
    pmax x1, blocking collectives, per_device(): row_max = lax.pmax(local_max, 'psg')  13.3 us
  transfers between devices with their start and end apart: 7, of which 6 were waited for; matrix products, arithmetic and copies ran while one was open for 32% of the time, Pallas kernels for 0%

profile of v1, /device:TPU:0, one launch (start us, length us, event | category | flops | bytes accessed | tf_op | source)
XLA Modules:
  0.0 579.4 jit_solution(10775751643776645967)
XLA Ops:
  7.2 0.7 all-gather.4.cloned.1.call-update
  7.9 5.5 stack.2
  13.4 5.3 all-to-all-start
  19.2 61.1 %while.21 = (s32[]{:T(128)}, bf16[4,512,1024]{2,1,0:T(8,128)(2,1)}, s32[4,512,128]{1,2,0:T(8,128)S(1)}, bf16[128,8,256]{2,1,0:T(8,128)(2,1)}, s32[]{:T(128)}) while((s32[]{:T(128)}, bf16[4,512,1024]{2,1,0:T(8,128)(2,1)}, s32[4,512,128]{1,2,0:T(8,128)S(1)}, bf16[128,8,256]{2,1,0:T(8,128)(2,1)}, s32[]{:T(128)}) %tuple.45), condition=%wide.region_2.3_spmd, body=%wide.region_1.2_spmd.sunk | while | flops 285736960 | bytes 6554177 | solution.py:42
  19.2 13.6 %fusion.47 = bf16[1,512,1024]{1,2,0:T(8,128)(2,1)S(1)} fusion(bf16[128,8,256]{2,1,0:T(8,128)(2,1)} %get-tuple-element.164, s32[512,128]{0,1:T(8,128)S(1)} %dynamic-slice_bitcast_fusion.4), kind=kOutput, calls=%fused_computation.4.clone.2 | convolution fusion | flops 285736960 | bytes 1835008 | tf_op jit(solution)/shard_map/while/body/eval_jaxpr/pmk,mdk->pmd/dot_general | solution.py:37
  32.9 0.5 copy.19
  33.4 1.1 constant_dynamic-update-slice_fusion.2
  34.5 13.6 %fusion.47 = bf16[1,512,1024]{1,2,0:T(8,128)(2,1)S(1)} fusion(bf16[128,8,256]{2,1,0:T(8,128)(2,1)} %get-tuple-element.164, s32[512,128]{0,1:T(8,128)S(1)} %dynamic-slice_bitcast_fusion.4), kind=kOutput, calls=%fused_computation.4.clone.2 | convolution fusion | flops 285736960 | bytes 1835008 | tf_op jit(solution)/shard_map/while/body/eval_jaxpr/pmk,mdk->pmd/dot_general | solution.py:37
  48.7 1.1 constant_dynamic-update-slice_fusion.2
  49.8 13.6 %fusion.47 = bf16[1,512,1024]{1,2,0:T(8,128)(2,1)S(1)} fusion(bf16[128,8,256]{2,1,0:T(8,128)(2,1)} %get-tuple-element.164, s32[512,128]{0,1:T(8,128)S(1)} %dynamic-slice_bitcast_fusion.4), kind=kOutput, calls=%fused_computation.4.clone.2 | convolution fusion | flops 285736960 | bytes 1835008 | tf_op jit(solution)/shard_map/while/body/eval_jaxpr/pmk,mdk->pmd/dot_general | solution.py:37
  63.9 1.1 constant_dynamic-update-slice_fusion.2
  65.0 13.6 %fusion.47 = bf16[1,512,1024]{1,2,0:T(8,128)(2,1)S(1)} fusion(bf16[128,8,256]{2,1,0:T(8,128)(2,1)} %get-tuple-element.164, s32[512,128]{0,1:T(8,128)S(1)} %dynamic-slice_bitcast_fusion.4), kind=kOutput, calls=%fused_computation.4.clone.2 | convolution fusion | flops 285736960 | bytes 1835008 | tf_op jit(solution)/shard_map/while/body/eval_jaxpr/pmk,mdk->pmd/dot_general | solution.py:37
  78.7 0.5 copy.19
  79.2 1.1 constant_dynamic-update-slice_fusion.2
  80.3 12.8 %all-gather.4.cloned.1.call-done = bf16[512,4096]{1,0:T(8,128)(2,1)} async-done(((bf16[128,4096]{1,0:T(8,128)(2,1)}), bf16[512,4096]{1,0:T(8,128)(2,1)}) %all-gather.4.cloned.1.call-update) | async-done | bytes 4194320 | tf_op jit(solution)/shard_map/all_gather | solution.py:16
  93.0 3.2 fusion.10
  96.5 3.5 fusion.12
  100.0 13.2 %all-to-all-done = bf16[8,512,1024]{2,1,0:T(8,128)(2,1)} async-done(((bf16[8,512,1024]{2,1,0:T(8,128)(2,1)}), bf16[8,512,1024]{2,1,0:T(8,128)(2,1)}, u32[]{:S(2)}, u32[]{:S(2)}) %all-to-all-start) | async-done | bytes 8388640 | tf_op jit(solution)/shard_map/all_to_all | solution.py:24
  113.3 9.3 %convolution_convert_fusion.1 = bf16[512,1024]{1,0:T(8,128)(2,1)S(1)} fusion(bf16[512,4096]{1,0:T(8,128)(2,1)} %fusion.12, bf16[4096,1024]{1,0:T(8,128)(2,1)} %bitcast.3), kind=kOutput, calls=%fused_computation.35 | convolution fusion | flops 4295491584 | bytes 13631488 | tf_op jit(solution)/shard_map/dot_general | solution.py:21
  122.5 1.0 copy-done.6
  123.5 4.3 convolution_multiply_fusion
  127.9 0.8 dynamic-slice_subtract_fusion
  128.7 76.3 %reduce-scatter.3.cloned.1.call-done = f32[128,2048]{1,0:T(8,128)} async-done(((f32[512,2048]{1,0:T(8,128)}), f32[128,2048]{1,0:T(8,128)}) %reduce-scatter.3.cloned.1.call-update) | async-done | bytes 1048592 | tf_op jit(solution)/shard_map/reduce_scatter | solution.py:51
  205.0 1.4 reduce_max.9
  206.3 13.3 %pmax.7 = f32[128]{0:T(128)S(1)} all-reduce(f32[128]{0:T(128)S(1)} %reduce_max.9), channel_id=1, replica_groups=mesh['psg'=8,'qry'=4] {'psg'}, use_global_device_ids=true, to_apply=%region_5.6 | all-reduce | flops 128 | bytes 1024 | tf_op jit(solution)/shard_map/pmax | solution.py:57
  219.6 1.6 fusion.20
  221.2 11.8 %psum.28 = f32[128]{0:T(128)S(1)} all-reduce(f32[128]{0:T(128)S(1)} %get-tuple-element.79), channel_id=1, replica_groups=mesh['psg'=8,'qry'=4] {'psg'}, use_global_device_ids=true, to_apply=%region_7.8 | all-reduce | flops 128 | bytes 1024 | tf_op jit(solution)/shard_map/psum | solution.py:59
  233.0 2.4 subtract_convert_fusion
  236.3 44.0 %all-gather.6.cloned.1.call-done = bf16[512,2048]{1,0:T(8,128)(2,1)} async-done(((bf16[128,2048]{1,0:T(8,128)(2,1)}), bf16[512,2048]{1,0:T(8,128)(2,1)}) %all-gather.6.cloned.1.call-update) | async-done | bytes 2097168 | tf_op jit(solution)/shard_map/all_gather | solution.py:64
  280.3 6.6 %convolution_multiply_fusion.1 = f32[512,1024]{1,0:T(8,128)} fusion(bf16[512,2048]{1,0:T(8,128)(2,1)} %all-gather.6.cloned.1.call-done, bf16[2048,1024]{1,0:T(8,128)(2,1)} %bitcast.44), kind=kOutput, calls=%fused_computation.34 | convolution fusion | flops 2148007936 | bytes 8388608 | tf_op jit(solution)/shard_map/dot_general | solution.py:65
  286.9 4.3 multiply_convert_fusion
  291.3 6.5 %copy.13 = bf16[2048,1024]{0,1:T(8,128)(2,1)} copy(bf16[2048,1024]{1,0:T(8,128)(2,1)} %multiply_convert_fusion) | data formatting | bytes 8388608 | tf_op jit(solution)/shard_map/convert_element_type | solution.py:72
  297.7 7.8 %reshape.55 = bf16[4,512,128,8]{1,0,3,2:T(4,128)(2,1)} reshape(bf16[2048,1024]{0,1:T(8,128)(2,1)} %copy.13) | data formatting | bytes 8388608 | tf_op jit(solution)/shard_map/reshape | solution.py:73
  305.6 5.0 copy.14
  310.6 66.8 %while.22 = (s32[]{:T(128)}, f32[128,8,256]{2,1,0:T(8,128)S(1)}, bf16[4,512,128,8]{1,3,2,0:T(8,128)(2,1)}, s32[4,512,128]{1,2,0:T(8,128)S(1)}, s32[]{:T(128)}, /*index=5*/s32[]{:T(128)}) while((s32[]{:T(128)}, f32[128,8,256]{2,1,0:T(8,128)S(1)}, bf16[4,512,128,8]{1,3,2,0:T(8,128)(2,1)}, s32[4,512,128]{1,2,0:T(8,128)S(1)}, ...), condition=%wide.region_15.16_spmd.clone, body=%wide.region_14.15_spmd.clone.sunk | while | flops 285736960 | bytes 3932755 | solution.py:86
  310.6 16.7 %fusion.49 = f32[128,8,256]{2,1,0:T(8,128)S(1)} fusion(s32[512,128]{0,1:T(8,128)S(1)} %dynamic-slice_bitcast_fusion.5, f32[128,8,256]{2,1,0:T(8,128)S(1)} %get-tuple-element.173, bf16[4,512,128,8]{1,3,2,0:T(8,128)(2,1)} %get-tuple-element.180, s32[]{:T(128)} %get-tuple-element.172, pred[]{:T(512)S(6)} %compare.3), kind=kOutput, calls=%fused_computation.10.clone.3 | convolution fusion | flops 285736960 | bytes 3408385 | tf_op jit(solution)/shard_map/while/body/eval_jaxpr/pmk,pmd->mdk/dot_general | solution.py:82
  327.3 16.7 %fusion.49 = f32[128,8,256]{2,1,0:T(8,128)S(1)} fusion(s32[512,128]{0,1:T(8,128)S(1)} %dynamic-slice_bitcast_fusion.5, f32[128,8,256]{2,1,0:T(8,128)S(1)} %get-tuple-element.173, bf16[4,512,128,8]{1,3,2,0:T(8,128)(2,1)} %get-tuple-element.180, s32[]{:T(128)} %get-tuple-element.172, pred[]{:T(512)S(6)} %compare.3), kind=kOutput, calls=%fused_computation.10.clone.3 | convolution fusion | flops 285736960 | bytes 3408385 | tf_op jit(solution)/shard_map/while/body/eval_jaxpr/pmk,pmd->mdk/dot_general | solution.py:82
  344.1 16.7 %fusion.49 = f32[128,8,256]{2,1,0:T(8,128)S(1)} fusion(s32[512,128]{0,1:T(8,128)S(1)} %dynamic-slice_bitcast_fusion.5, f32[128,8,256]{2,1,0:T(8,128)S(1)} %get-tuple-element.173, bf16[4,512,128,8]{1,3,2,0:T(8,128)(2,1)} %get-tuple-element.180, s32[]{:T(128)} %get-tuple-element.172, pred[]{:T(512)S(6)} %compare.3), kind=kOutput, calls=%fused_computation.10.clone.3 | convolution fusion | flops 285736960 | bytes 3408385 | tf_op jit(solution)/shard_map/while/body/eval_jaxpr/pmk,pmd->mdk/dot_general | solution.py:82
  360.8 16.7 %fusion.49 = f32[128,8,256]{2,1,0:T(8,128)S(1)} fusion(s32[512,128]{0,1:T(8,128)S(1)} %dynamic-slice_bitcast_fusion.5, f32[128,8,256]{2,1,0:T(8,128)S(1)} %get-tuple-element.173, bf16[4,512,128,8]{1,3,2,0:T(8,128)(2,1)} %get-tuple-element.180, s32[]{:T(128)} %get-tuple-element.172, pred[]{:T(512)S(6)} %compare.3), kind=kOutput, calls=%fused_computation.10.clone.3 | convolution fusion | flops 285736960 | bytes 3408385 | tf_op jit(solution)/shard_map/while/body/eval_jaxpr/pmk,pmd->mdk/dot_general | solution.py:82
  377.4 0.8 convert_element_type.58
  378.3 57.9 %all-reduce.5 = (f32[128]{0:T(128)S(1)}, bf16[512,1024]{1,0:T(8,128)(2,1)S(1)}) all-reduce(f32[128]{0:T(128)S(1)} %get-tuple-element.80, f32[512,1024]{1,0:T(8,128)} %convolution_multiply_fusion.1), channel_id=1, replica_groups=mesh['psg'=8,'qry'=4] {'psg'}, use_global_device_ids=true, to_apply=%region_9.10 | all-reduce | flops 524416 | bytes 3146752 | tf_op jit(solution)/shard_map/psum | solution.py:59
  436.3 9.4 %convolution_convert_fusion = bf16[512,4096]{1,0:T(8,128)(2,1)} fusion(bf16[4096,1024]{1,0:T(8,128)(2,1)} %all-gather.8.cloned.1.call-done, bf16[512,1024]{1,0:T(8,128)(2,1)S(1)} %get-tuple-element.98), kind=kOutput, calls=%fused_computation.21 | convolution fusion | flops 4297064448 | bytes 13631488 | tf_op jit(solution)/shard_map/dot_general | solution.py:95
  446.3 3.1 fusion.21
  449.4 40.1 %all-reduce.4.cloned.1.call-done = bf16[128,8,256]{2,1,0:T(8,128)(2,1)} async-done(((bf16[128,8,256]{2,1,0:T(8,128)(2,1)}), bf16[128,8,256]{2,1,0:T(8,128)(2,1)}) %all-reduce.4.cloned.1.call-update) | async-done | bytes 524304 | tf_op jit(solution)/shard_map/psum | solution.py:89
  489.6 2.1 convert_element_type.59
  491.6 76.2 %reduce-scatter.5.cloned.1.call-done = bf16[128,4096]{1,0:T(8,128)(2,1)} async-done(((bf16[512,4096]{1,0:T(8,128)(2,1)}), bf16[128,4096]{1,0:T(8,128)(2,1)}) %reduce-scatter.5.cloned.1.call-update) | async-done | bytes 1048592 | tf_op jit(solution)/shard_map/reduce_scatter | solution.py:101
  567.8 1.8 fusion.13
  569.6 2.9 fusion.18
  (43 shorter events, 3.4 us)
Async XLA Ops:
  7.2 85.9 %all-gather.4.cloned.1.call-start = ((), (), s32[]{:S(2)}) async-start(), calls=%async_computation.3 | async-start | bytes 5242880 | tf_op jit(solution)/shard_map/all_gather | solution.py:16
  13.4 5.4 copy-start.2
  13.4 99.8 %all-to-all-start = ((bf16[8,512,1024]{2,1,0:T(8,128)(2,1)}), bf16[8,512,1024]{2,1,0:T(8,128)(2,1)}, u32[]{:S(2)}, u32[]{:S(2)}) async-start(bf16[8,512,1024]{2,1,0:T(8,128)(2,1)} %stack.2), calls=%async_computation | async-start | bytes 16777216 | tf_op jit(solution)/shard_map/all_to_all | solution.py:24
  18.8 186.2 %reduce-scatter.3.cloned.1.call-start = ((), (), s32[]{:S(2)}) async-start(), calls=%async_computation.4 | async-start | bytes 5242880 | tf_op jit(solution)/shard_map/reduce_scatter | solution.py:51
  19.2 77.1 %copy-start.3 = (f32[4096]{0:T(1024)S(1)}, f32[4096]{0:T(1024)}, u32[]{:S(2)}) copy-start(f32[4096]{0:T(1024)} %param.11) | copy-start | bytes 49156
  93.0 3.4 copy-start
  113.3 10.3 %copy-start.4 = (bf16[4,512,1024]{2,1,0:T(8,128)(2,1)S(1)}, bf16[4,512,1024]{2,1,0:T(8,128)(2,1)}, u32[]{:S(2)}) copy-start(bf16[4,512,1024]{2,1,0:T(8,128)(2,1)} %get-tuple-element.48) | copy-start | bytes 12582916
  122.5 1.0 copy-start.6
  127.8 152.4 %all-gather.6.cloned.1.call-start = ((), (), s32[]{:S(2)}) async-start(), calls=%async_computation.5 | async-start | bytes 2621440 | tf_op jit(solution)/shard_map/all_gather | solution.py:64
  235.5 200.8 %all-gather.8.cloned.1.call-start = ((), (), s32[]{:S(2)}) async-start(), calls=%async_computation.6 | async-start | bytes 9437184 | tf_op jit(solution)/shard_map/all_gather | solution.py:97
  236.1 253.5 %all-reduce.4.cloned.1.call-start = ((), (), s32[]{:S(2)}) async-start(), calls=%async_computation.8 | async-start | bytes 1048576 | tf_op jit(solution)/shard_map/psum | solution.py:89
  280.3 6.6 %copy-start.5 = (bf16[512,2048]{1,0:T(8,128)(2,1)S(1)}, bf16[512,2048]{1,0:T(8,128)(2,1)}, u32[]{:S(2)}) copy-start(bf16[512,2048]{1,0:T(8,128)(2,1)} %all-gather.6.cloned.1.call-done) | copy-start | bytes 6291460
  280.3 6.6 %copy-start.7 = (bf16[512,1024]{1,0:T(8,128)(2,1)S(1)}, bf16[512,1024]{1,0:T(8,128)(2,1)}, u32[]{:S(2)}) copy-start(bf16[512,1024]{1,0:T(8,128)(2,1)} %copy-done.6) | copy-start | bytes 3145732
  436.2 131.6 %reduce-scatter.5.cloned.1.call-start = ((), (), s32[]{:S(2)}) async-start(), calls=%async_computation.7 | async-start | bytes 5242880 | tf_op jit(solution)/shard_map/reduce_scatter | solution.py:101
  445.8 122.0 %copy-start.1 = (bf16[128,4096]{1,0:T(8,128)(2,1)S(1)}, bf16[128,4096]{1,0:T(8,128)(2,1)}, u32[]{:S(2)}) copy-start(bf16[128,4096]{1,0:T(8,128)(2,1)} %param.10) | copy-start | bytes 3145732
Sparse Core Ops, SparseCore 0:
  9.5 83.4 all-gather.3
  128.0 76.9 reduce-scatter.2
  235.6 44.6 all-gather.5
  282.0 53.1 all-gather.7
  436.4 53.1 all-reduce.3
  491.7 76.0 reduce-scatter.4
